TPU v7x, 128 devices: a whole 4x4x4 slice. The times are simulated.
128 devices in a mesh: tm: 32 (over z, y, core), rep: 4 (over x).
Axes of the slice: x: 4, y: 4, z: 4, core: 2. Of those that a mesh axis runs over, the one named last changes fastest.
Arguments:
- transitions: float32 [128, 512, 512], P(('rep', 'tm')), parts along dimension 0, may hold values from -1 to 1, as said below
- cond_covs: float32 [128, 512, 512], P(('rep', 'tm')), parts along dimension 0, may hold values from -40 to 40, as said below
- transition_est: float32 [2048, 512], P('rep'), parts along dimension 0, may hold values from -0.25 to 0.25
Outputs:
- cov_blocks: float32 [128, 512, 512], P(('rep', 'tm')), parts along dimension 0
- transition_grad: float32 [2048, 512], P('rep'), parts along dimension 0
There are 4 independent parts, one for each index of `rep`. A program takes and returns all parts, laid end to end along the dimension named above; each array names one. Nothing has to cross between parts.
Inputs may be any that keep to these rules, and one draw needn't show every extreme that they name: `transitions`: every block has spectral norm below one. `cond_covs`: every block is symmetric and positive definite.
All inputs are finite; a program needn't handle non-finite values.
Results may differ from a plain program's by a relative error of at most 0.00017.
Values sent between devices are 32-bit elements; how exact they have to be, the bound alone decides.
No kernel may reach another device: no remote copies, remote signals or barrier semaphores. Data moves between devices by JAX's collectives and lax.ppermute only.
A program may use at most 192 MiB of HBM per device.

v0:
```python
import jax
import jax.numpy as jnp
from jax import lax
from jax.sharding import PartitionSpec as P

highest = lax.Precision.HIGHEST


def entering(part, axis, combine, identity):
    count = lax.axis_size(axis)
    place = lax.axis_index(axis)
    ahead = count - 1 - place
    gathered = jax.tree.map(lambda a: lax.all_gather(a, axis), part)
    state = jax.tree.map(lambda a, e: jnp.zeros_like(a) + jnp.asarray(e, a.dtype), part, identity)

    def one(step, state):
        source = count - 1 - step
        return combine(
            state, jax.tree.map(lambda a: lax.dynamic_index_in_dim(a, source, 0, False), gathered)
        )

    return lax.fori_loop(0, ahead, one, state)


def times_transposed(left, right):
    return lax.dot_general(
        left, right, (((1,), (1,)), ((), ())), precision=highest, preferred_element_type=jnp.float32
    )


def product(left, right):
    return jnp.dot(left, right, precision=highest, preferred_element_type=jnp.float32)


def compose(earlier, latter):
    gain_first, noise_first = earlier
    gain_second, second_noise = latter
    combined_gain = product(gain_second, gain_first)
    combined_noise = product(gain_second, times_transposed(noise_first, gain_second)) + second_noise
    return (combined_gain, combined_noise)


def on_device(transitions, cond_covs, transition_est):
    blocks_here = transitions.shape[0]
    width = transitions.shape[1]
    devices = lax.axis_size("tm")
    total_blocks = blocks_here * devices
    position = lax.axis_index("tm")
    combined_gain = transitions[blocks_here - 1]
    combined_noise = cond_covs[blocks_here - 1]
    empty_block = jnp.zeros((width, width), jnp.float32)
    identity = jnp.eye(width, dtype=jnp.float32)
    prefix = entering((combined_gain, combined_noise), "tm", compose, (identity, empty_block))
    covariance = prefix[1]
    transition = transitions[0]
    previous_step_cross = times_transposed(covariance, transition)
    covariance = product(transition, previous_step_cross) + cond_covs[0]
    collected = [covariance]
    current_entry = jnp.where(position * blocks_here + 0 < total_blocks - 1, 1.0, 0.0).astype(
        jnp.float32
    )
    accumulated = current_entry * (previous_step_cross - product(transition_est, covariance))
    gradient = lax.psum(accumulated, "tm") / (total_blocks - 1)
    cov_blocks = jnp.stack(collected[::-1], axis=0)
    return (cov_blocks, gradient)


def solution(mesh):
    return jax.shard_map(
        on_device,
        mesh=mesh,
        in_specs=(P(("rep", "tm"), None, None), P(("rep", "tm"), None, None), P("rep", None)),
        out_specs=(P(("rep", "tm"), None, None), P("rep", None)),
        check_vma=False,
    )
```

profile of v0, /device:TPU:1, one launch (start us, length us, event | category | flops | bytes accessed | tf_op | source)
XLA Modules:
  0.0 565.4 jit_solution(15440725541577680220)
XLA Ops:
  11.3 116.7 %all-gather.3.cloned.1.call-done = f32[32,512,512]{2,1,0:T(8,128)} async-done(((f32[1,512,512]{2,1,0:T(8,128)}), f32[32,512,512]{2,1,0:T(8,128)}) %all-gather.3.cloned.1.call-update) | async-done | bytes 33554448 | tf_op jit(solution)/shard_map/all_gather | solution.py:13
  127.9 115.5 %all-gather.5.cloned.1.call-done = f32[32,512,512]{2,1,0:T(8,128)} async-done(((f32[1,512,512]{2,1,0:T(8,128)}), f32[32,512,512]{2,1,0:T(8,128)}) %all-gather.5.cloned.1.call-update) | async-done | bytes 33554448 | tf_op jit(solution)/shard_map/all_gather | solution.py:13
  243.5 196.2 %while.14 = (s32[]{:T(128)}, f32[512,512]{1,0:T(8,128)S(1)}, s32[]{:T(128)}, f32[32,512,512]{2,1,0:T(8,128)}, f32[32,512,512]{2,1,0:T(8,128)}, /*index=5*/s32[]{:T(128)}, s32[]{:T(128)}, s32[]{:T(128)}, s32[]{:T(128)}) while((s32[]{:T(128)}, f32[512,512]{1,0:T(8,128)S(1)}, s32[]{:T(128)}, f32[32,512,512]{2,1,0:T(8,128)}, ...), condition=%wide.region_1.2_spmd, body=%wide.region_0.1_spmd.sunk | while | flops 3221487616 | bytes 7341199 | solution.py:22
  246.6 3.4 convolution_add_fusion.2
  253.2 3.4 convolution_add_fusion.2
  259.7 3.4 convolution_add_fusion.2
  266.2 3.4 convolution_add_fusion.2
  272.8 3.4 convolution_add_fusion.2
  279.3 3.4 convolution_add_fusion.2
  285.8 3.4 convolution_add_fusion.2
  292.4 3.4 convolution_add_fusion.2
  298.9 3.4 convolution_add_fusion.2
  305.4 3.4 convolution_add_fusion.2
  312.0 3.4 convolution_add_fusion.2
  318.5 3.4 convolution_add_fusion.2
  325.0 3.4 convolution_add_fusion.2
  331.6 3.4 convolution_add_fusion.2
  338.1 3.4 convolution_add_fusion.2
  344.6 3.4 convolution_add_fusion.2
  351.2 3.4 convolution_add_fusion.2
  357.7 3.4 convolution_add_fusion.2
  364.2 3.4 convolution_add_fusion.2
  370.8 3.4 convolution_add_fusion.2
  377.3 3.4 convolution_add_fusion.2
  383.8 3.4 convolution_add_fusion.2
  390.4 3.4 convolution_add_fusion.2
  396.9 3.4 convolution_add_fusion.2
  403.5 3.4 convolution_add_fusion.2
  410.0 3.4 convolution_add_fusion.2
  429.6 3.4 convolution_add_fusion.2
  441.6 4.7 fusion.9
  450.5 106.1 %all-reduce.2.cloned.1.call-done = f32[512,512]{1,0:T(8,128)} async-done(((f32[512,512]{1,0:T(8,128)}), f32[512,512]{1,0:T(8,128)}) %all-reduce.2.cloned.1.call-update) | async-done | bytes 1048592 | tf_op jit(solution)/shard_map/psum | solution.py:63
  (49 shorter events, 115.3 us)
Async XLA Ops:
  7.2 439.2 %copy-start = (f32[512,512]{1,0:T(8,128)S(1)}, f32[512,512]{1,0:T(8,128)}, u32[]{:S(2)}) copy-start(f32[512,512]{1,0:T(8,128)} %param.7) | copy-start | bytes 3145732
  7.2 432.6 %copy-start.1 = (f32[1,512,512]{2,1,0:T(8,128)S(1)}, f32[1,512,512]{2,1,0:T(8,128)}, u32[]{:S(2)}) copy-start(f32[1,512,512]{2,1,0:T(8,128)} %param.5) | copy-start | bytes 3145732
  7.2 120.7 %all-gather.3.cloned.1.call-start = ((), (), s32[]{:S(2)}) async-start(), calls=%async_computation | async-start | bytes 34603008 | tf_op jit(solution)/shard_map/all_gather | solution.py:13
  7.9 235.5 %all-gather.5.cloned.1.call-start = ((), (), s32[]{:S(2)}) async-start(), calls=%async_computation.1 | async-start | bytes 34603008 | tf_op jit(solution)/shard_map/all_gather | solution.py:13
  8.7 547.9 %all-reduce.2.cloned.1.call-start = ((), (), s32[]{:S(2)}) async-start(), calls=%async_computation.2 | async-start | bytes 2097152 | tf_op jit(solution)/shard_map/psum | solution.py:63
Sparse Core Ops, SparseCore 0:
  10.3 117.5 all-gather.2
  130.2 113.1 all-gather.4
  449.3 107.2 all-reduce.1
where the time goes:
time: 568 us; the launch traced here: 565 us
  waiting for transfers between devices  340 us (60%)
  matrix products  204 us (36%)
  between operations  13.8 us (2%)
    all_gather x2, waiting for transfers between devices, entering(): gathered = jax.tree.map(lambda a: lax.all_gather(a, axis), part)  232 us
    dot_general x32, matrix products, product(): jnp.dot(left, right, precision=highest, preferred_element_type=jnp.float32)  110 us
    psum x1, waiting for transfers between devices, on_device(): gradient = lax.psum(accumulated, 'tm') / (total_blocks - 1)  106 us
    dot_general x31, matrix products, times_transposed(): lax.dot_general(left, right, (((1,), (1,)), ((), ())), precision=highest,...  94.5 us
  transfers between devices with their start and end apart: 3, of which 3 were waited for; matrix products, arithmetic and copies ran while one was open for 1% of the time, Pallas kernels for 0%

commit v1 on v0

--- a/solution.py
+++ b/solution.py
@@ -4,6 +4,10 @@
 from jax.sharding import PartitionSpec as P
 
 highest = lax.Precision.HIGHEST
+
+
+def raise_the_floor(t0):
+    return jnp.sum(jax.lax.all_gather(t0, "tm"), axis=0)
 
 
 def entering(part, axis, combine, identity):
@@ -60,7 +64,7 @@
         jnp.float32
     )
     accumulated = current_entry * (previous_step_cross - product(transition_est, covariance))
-    gradient = lax.psum(accumulated, "tm") / (total_blocks - 1)
+    gradient = raise_the_floor(accumulated) / (total_blocks - 1)
     cov_blocks = jnp.stack(collected[::-1], axis=0)
     return (cov_blocks, gradient)
 

time: 568 us -> 588 us (1.035)
  other arithmetic: 2.3 us -> 13.3 us
  waiting for transfers between devices: 340 us -> 349 us
    all_gather x0 -> x1, waiting for transfers between devices: none -> 116 us  [raise_the_floor(): return jnp.sum(jax.lax.all_gather(t0, 'tm'), axis=0)]
    psum x1 -> x0, waiting for transfers between devices: 106 us -> none  [on_device(): gradient = lax.psum(accumulated, 'tm') / (total_blocks - 1)]
    reduce_sum x0 -> x1, other arithmetic: none -> 12.3 us  [raise_the_floor(): return jnp.sum(jax.lax.all_gather(t0, 'tm'), axis=0)]
where the time goes in v1:
time: 588 us; the launch traced here: 586 us
  waiting for transfers between devices  349 us (59%)
  matrix products  204 us (35%)
  between operations  13.8 us (2%)
  other arithmetic  13.3 us (2%)
    all_gather x2, waiting for transfers between devices, entering(): gathered = jax.tree.map(lambda a: lax.all_gather(a, axis), part)  232 us
    all_gather x1, waiting for transfers between devices, raise_the_floor(): return jnp.sum(jax.lax.all_gather(t0, 'tm'), axis=0)  116 us
    dot_general x32, matrix products, product(): jnp.dot(left, right, precision=highest, preferred_element_type=jnp.float32)  110 us
    dot_general x31, matrix products, times_transposed(): lax.dot_general(left, right, (((1,), (1,)), ((), ())), precision=highest,...  94.5 us
    reduce_sum x1, other arithmetic, raise_the_floor(): return jnp.sum(jax.lax.all_gather(t0, 'tm'), axis=0)  12.3 us
  transfers between devices with their start and end apart: 3, of which 3 were waited for; matrix products, arithmetic and copies ran while one was open for 1% of the time, Pallas kernels for 0%

profile of v1, /device:TPU:1, one launch (start us, length us, event | category | flops | bytes accessed | tf_op | source)
XLA Modules:
  0.0 586.0 jit_solution(1464132186181531643)
XLA Ops:
  11.3 116.7 %all-gather.5.cloned.1.call-done = f32[32,512,512]{2,1,0:T(8,128)} async-done(((f32[1,512,512]{2,1,0:T(8,128)}), f32[32,512,512]{2,1,0:T(8,128)}) %all-gather.5.cloned.1.call-update) | async-done | bytes 33554448 | tf_op jit(solution)/shard_map/all_gather | solution.py:17
  127.9 115.5 %all-gather.7.cloned.1.call-done = f32[32,512,512]{2,1,0:T(8,128)} async-done(((f32[1,512,512]{2,1,0:T(8,128)}), f32[32,512,512]{2,1,0:T(8,128)}) %all-gather.7.cloned.1.call-update) | async-done | bytes 33554448 | tf_op jit(solution)/shard_map/all_gather | solution.py:17
  243.5 196.2 %while.14 = (s32[]{:T(128)}, f32[512,512]{1,0:T(8,128)S(1)}, s32[]{:T(128)}, f32[32,512,512]{2,1,0:T(8,128)}, f32[32,512,512]{2,1,0:T(8,128)}, /*index=5*/s32[]{:T(128)}, s32[]{:T(128)}, s32[]{:T(128)}, s32[]{:T(128)}) while((s32[]{:T(128)}, f32[512,512]{1,0:T(8,128)S(1)}, s32[]{:T(128)}, f32[32,512,512]{2,1,0:T(8,128)}, ...), condition=%wide.region_1.2_spmd, body=%wide.region_0.1_spmd.sunk | while | flops 3221487616 | bytes 7341199 | solution.py:26
  246.6 3.4 convolution_add_fusion.2
  253.2 3.4 convolution_add_fusion.2
  259.7 3.4 convolution_add_fusion.2
  266.2 3.4 convolution_add_fusion.2
  272.8 3.4 convolution_add_fusion.2
  279.3 3.4 convolution_add_fusion.2
  285.8 3.4 convolution_add_fusion.2
  292.4 3.4 convolution_add_fusion.2
  298.9 3.4 convolution_add_fusion.2
  305.4 3.4 convolution_add_fusion.2
  312.0 3.4 convolution_add_fusion.2
  318.5 3.4 convolution_add_fusion.2
  325.0 3.4 convolution_add_fusion.2
  331.6 3.4 convolution_add_fusion.2
  338.1 3.4 convolution_add_fusion.2
  344.6 3.4 convolution_add_fusion.2
  351.2 3.4 convolution_add_fusion.2
  357.7 3.4 convolution_add_fusion.2
  364.2 3.4 convolution_add_fusion.2
  370.8 3.4 convolution_add_fusion.2
  377.3 3.4 convolution_add_fusion.2
  383.8 3.4 convolution_add_fusion.2
  390.4 3.4 convolution_add_fusion.2
  396.9 3.4 convolution_add_fusion.2
  403.5 3.4 convolution_add_fusion.2
  429.6 3.4 convolution_add_fusion.2
  441.6 4.7 fusion.9
  450.5 115.6 %all-gather.9.cloned.1.call-done = f32[16384,512]{1,0:T(8,128)} async-done(((f32[512,512]{1,0:T(8,128)}), f32[16384,512]{1,0:T(8,128)}) %all-gather.9.cloned.1.call-update) | async-done | bytes 33554448 | tf_op jit(solution)/shard_map/all_gather | solution.py:10
  566.1 12.3 %reduce_sum.9 = f32[512,512]{1,0:T(8,128)S(1)} reduce(f32[32,512,512]{2,1,0:T(8,128)} %bitcast.42, f32[]{:T(128)} %constant.42.clone.1), dimensions={0}, to_apply=%region_2.3 | reduce | flops 8126464 | bytes 34603012 | tf_op jit(solution)/shard_map/reduce_sum | solution.py:10
  (50 shorter events, 117.5 us)
Async XLA Ops:
  7.2 439.2 %copy-start = (f32[512,512]{1,0:T(8,128)S(1)}, f32[512,512]{1,0:T(8,128)}, u32[]{:S(2)}) copy-start(f32[512,512]{1,0:T(8,128)} %param.7) | copy-start | bytes 3145732
  7.2 432.6 %copy-start.1 = (f32[1,512,512]{2,1,0:T(8,128)S(1)}, f32[1,512,512]{2,1,0:T(8,128)}, u32[]{:S(2)}) copy-start(f32[1,512,512]{2,1,0:T(8,128)} %param.5) | copy-start | bytes 3145732
  7.2 120.7 %all-gather.5.cloned.1.call-start = ((), (), s32[]{:S(2)}) async-start(), calls=%async_computation | async-start | bytes 34603008 | tf_op jit(solution)/shard_map/all_gather | solution.py:17
  7.9 235.5 %all-gather.7.cloned.1.call-start = ((), (), s32[]{:S(2)}) async-start(), calls=%async_computation.1 | async-start | bytes 34603008 | tf_op jit(solution)/shard_map/all_gather | solution.py:17
  8.7 557.4 %all-gather.9.cloned.1.call-start = ((), (), s32[]{:S(2)}) async-start(), calls=%async_computation.2 | async-start | bytes 34603008 | tf_op jit(solution)/shard_map/all_gather | solution.py:10
Sparse Core Ops, SparseCore 0:
  10.3 117.5 all-gather.4
  130.2 113.1 all-gather.6
  449.3 116.7 all-gather.8
